TPU v7x, 32 devices: a whole 2x2x4 slice. The times are simulated.
32 devices in a mesh: row: 2 (over x), col: 16 (over z, y, core).
Axes of the slice: x: 2, y: 2, z: 4, core: 2. Of those that a mesh axis runs over, the one named last changes fastest.
Arguments:
- coords: float32 [64, 3, 256], P(('row', 'col')), may hold values from 0 to 8, as said below
- noise_var: float32 [64, 256], P(('row', 'col')), may hold values from 0.1 to 1
- right_side: float32 [64, 8, 256], P(('row', 'col')), may hold values from -32 to 32
- start_guess: float32 [64, 8, 256], P(('row', 'col')), may hold values from -3 to 3
- tile_pairs: int32 [2, 16, 2, 63], P('row', 'col'), may hold values from -1 to 31, as said below
Outputs:
- solution_field: float32 [64, 8, 256], P(('row', 'col'))
- residual: float32 [64, 8, 256], P(('row', 'col'))
Inputs may be any that keep to these rules, and one draw needn't show every extreme that they name: `coords`: each tile's points lie within one unit cell of the integer lattice, and distinct tiles lie in distinct cells. `tile_pairs`: each device's list holds every pair of its block whose cells differ by at most one in each coordinate, each pair once and no other; listed entries come first, then entries of -1 in both rows.
All inputs are finite; a program needn't handle non-finite values.
Results may differ from a plain program's by a relative error of at most 0.0003.
Values sent between devices are 32-bit elements; how exact they have to be, the bound alone decides.
A program may use at most 64 MiB of HBM per device.

v0:
```python
import jax
import jax.numpy as jnp
from jax import lax
from jax.sharding import PartitionSpec as P

ITERS = 3


pair_group = 2


def wendland(left_points, right_points):
    squared = jnp.zeros(
        (left_points.shape[0], left_points.shape[2], right_points.shape[2]), jnp.float32
    )
    for component in range(3):
        spacing = left_points[:, component, :, None] - right_points[:, component, None, :]
        squared = squared + spacing * spacing
    distance = jnp.sqrt(squared)
    remain = jnp.maximum(1.0 - distance, 0.0)
    return remain**4 * (4.0 * distance + 1.0)


def squares(residual):
    return lax.psum(jnp.sum(residual * residual, axis=(0, 2)), ("row", "col"))


def shards(coords, noise_var, right_side, start_guess, tile_pairs):
    row_points = lax.all_gather(coords, "col", axis=0, tiled=True)
    col_points = lax.all_gather(coords, "row", axis=0, tiled=True)
    row_count = row_points.shape[0]
    listed = tile_pairs[0, 0]
    usable = listed[0] >= 0
    sort_key = jnp.where(usable, listed[0], row_count)
    sorted_index = jnp.argsort(sort_key, stable=True)
    sorted_rows = jnp.concatenate(
        [sort_key[sorted_index], jnp.full((pair_group,), row_count, jnp.int32)]
    )
    sorted_cols = jnp.concatenate(
        [jnp.where(usable, listed[1], 0)[sorted_index], jnp.zeros((pair_group,), jnp.int32)]
    )

    def pair_range(first_row, row_number):
        first = jnp.sum(sorted_rows < first_row)
        last = jnp.sum(sorted_rows < first_row + row_number)
        return (first, last, (last - first + pair_group - 1) // pair_group)

    def group_weights(position, last):
        indices = position + jnp.arange(pair_group, dtype=jnp.int32)
        rows_group = lax.dynamic_slice_in_dim(sorted_rows, position, pair_group)
        cols_group = lax.dynamic_slice_in_dim(sorted_cols, position, pair_group)
        inside = (indices < last).astype(jnp.float32)
        safe_rows = jnp.minimum(rows_group, row_count - 1)
        weights = wendland(row_points[safe_rows], col_points[cols_group]) * inside[:, None, None]
        return (weights, safe_rows, cols_group)

    def apply_operator(vectors):
        empty = jnp.zeros((col_points.shape[0],) + vectors.shape[1:], jnp.float32)
        pieces = lax.all_gather(vectors, "col", axis=0, tiled=True)
        number = pieces.shape[0]
        first, last, turns = pair_range(jnp.int32(0), number)

        def visit(turn, running):
            weights, safe_rows, cols_group = group_weights(first + pair_group * turn, last)
            local_rows = jnp.clip(safe_rows, 0, number - 1)
            product = jnp.einsum(
                "pab,psa->psb", weights, pieces[local_rows], precision=lax.Precision.HIGHEST
            )
            return running.at[cols_group].add(product)

        gathered_sum = lax.fori_loop(0, turns, visit, empty)
        coupled = lax.psum_scatter(gathered_sum, "row", scatter_dimension=0, tiled=True)
        return coupled + noise_var[:, None, :] * vectors

    solution_field = start_guess
    residual = right_side - apply_operator(start_guess)
    direction = residual
    norm_now = squares(residual)
    for iteration in range(ITERS):
        applied = apply_operator(direction)
        step_size = norm_now / lax.psum(jnp.sum(direction * applied, axis=(0, 2)), ("row", "col"))
        solution_field = solution_field + step_size[None, :, None] * direction
        residual = residual - step_size[None, :, None] * applied
        norm_next = squares(residual)
        direction = residual + (norm_next / norm_now)[None, :, None] * direction
        norm_now = norm_next
    return (solution_field, residual)


def solution(mesh):
    placed = (
        P(("row", "col"), None, None),
        P(("row", "col"), None),
        P(("row", "col"), None, None),
        P(("row", "col"), None, None),
        P("row", "col", None, None),
    )
    return jax.shard_map(
        shards,
        mesh=mesh,
        in_specs=placed,
        out_specs=(P(("row", "col"), None, None), P(("row", "col"), None, None)),
        check_vma=False,
    )
```

profile of v0, /device:TPU:0, one launch (start us, length us, event | category | flops | bytes accessed | tf_op | source)
XLA Modules:
  0.0 645.9 jit_solution(4284149621219089081)
XLA Ops:
  8.0 2.0 sort.17
  13.5 23.5 %all_gather.19 = f32[32,3,256]{2,1,0:T(4,128)S(1)} all-gather(f32[2,3,256]{2,1,0:T(4,128)S(1)} %copy.11), channel_id=1, replica_groups=mesh['row'=2,'col'=16] {'col'}, dimensions={0}, use_global_device_ids=true | all-gather | bytes 104448 | tf_op jit(solution)/shard_map/all_gather | solution.py:29
  36.9 4.3 all_gather.20
  42.1 17.8 %all_gather.18 = f32[32,8,256]{2,1,0:T(8,128)S(1)} all-gather(f32[2,8,256]{2,1,0:T(8,128)S(1)} %copy-done.5), channel_id=1, replica_groups=mesh['row'=2,'col'=16] {'col'}, dimensions={0}, use_global_device_ids=true | all-gather | bytes 278528 | tf_op jit(solution)/shard_map/all_gather | solution.py:59
  59.9 69.6 %while.40 = (s32[]{:T(128)}, f32[4,8,256]{2,1,0:T(8,128)S(1)}, s32[]{:T(128)}, s32[]{:T(128)}, s32[65]{0:T(128)S(1)}, /*index=5*/s32[65]{0:T(128)S(1)}, f32[32,8...) while((s32[]{:T(128)}, f32[4,8,256]{2,1,0:T(8,128)S(1)}, ...), condition=%wide.region_5.6_spmd, body=%wide.region_3.5_spmd.sunk | while | flops 14687269 | bytes 213307 | solution.py:71
  128.1 0.8 fusion.162
  130.3 8.7 %reduce-scatter.5.cloned.1.call-done = f32[2,8,256]{2,1,0:T(8,128)} async-done(((f32[4,8,256]{2,1,0:T(8,128)}), f32[2,8,256]{2,1,0:T(8,128)}) %reduce-scatter.5.cloned.1.call-update) | async-done | bytes 16400 | tf_op jit(solution)/shard_map/reduce_scatter | solution.py:72
  139.7 22.0 %all_gather.21 = f32[32,8,256]{2,1,0:T(8,128)S(1)} all-gather(f32[2,8,256]{2,1,0:T(8,128)S(1)} %add_subtract_fusion), channel_id=1, replica_groups=mesh['row'=2,'col'=16] {'col'}, dimensions={0}, use_global_device_ids=true | all-gather | bytes 278528 | tf_op jit(solution)/shard_map/all_gather | solution.py:59
  161.8 69.7 %while.41 = (s32[]{:T(128)}, f32[4,8,256]{2,1,0:T(8,128)S(1)}, s32[]{:T(128)}, s32[]{:T(128)}, s32[65]{0:T(128)S(1)}, /*index=5*/s32[65]{0:T(128)S(1)}, f32[32,8...) while((s32[]{:T(128)}, f32[4,8,256]{2,1,0:T(8,128)S(1)}, ...), condition=%wide.region_11.12_spmd, body=%wide.region_9.11_spmd.sunk | while | flops 14687269 | bytes 213307 | solution.py:71
  165.0 0.8 fusion.167
  169.6 0.8 fusion.167
  174.2 0.8 fusion.167
  178.9 0.8 fusion.167
  183.5 0.8 fusion.167
  202.1 0.8 fusion.167
  211.4 0.8 fusion.167
  216.0 0.8 fusion.167
  220.7 0.8 fusion.167
  225.3 0.8 fusion.167
  232.1 6.3 reduce-scatter.7.cloned.1.call-done
  238.4 0.9 multiply_reduce_fusion.4
  239.4 39.3 %all-reduce.2 = (f32[8]{0:T(128)S(1)}, f32[8]{0:T(128)S(1)}) all-reduce(f32[8]{0:T(128)S(1)} %get-tuple-element.221, f32[8]{0:T(128)S(1)} %get-tuple-element.220), channel_id=1, replica_groups=mesh['row'=2,'col'=16] {'row','col'}, use_global_device_ids=true, to_apply=%region_8.9 | all-reduce | flops 16 | bytes 128 | tf_op jit(solution)/shard_map/psum | solution.py:25
  278.9 41.0 %psum.44 = f32[8]{0:T(128)S(1)} all-reduce(f32[8]{0:T(128)S(1)} %multiply_reduce_fusion.3), channel_id=1, replica_groups=mesh['row'=2,'col'=16] {'row','col'}, use_global_device_ids=true, to_apply=%region_16.17 | all-reduce | flops 8 | bytes 64 | tf_op jit(solution)/shard_map/psum | solution.py:25
  320.0 21.8 %all_gather.22 = f32[32,8,256]{2,1,0:T(8,128)S(1)} all-gather(f32[2,8,256]{2,1,0:T(8,128)S(1)} %multiply_add_fusion.4), channel_id=1, replica_groups=mesh['row'=2,'col'=16] {'col'}, dimensions={0}, use_global_device_ids=true | all-gather | bytes 278528 | tf_op jit(solution)/shard_map/all_gather | solution.py:59
  341.8 69.7 %while.42 = (s32[]{:T(128)}, f32[4,8,256]{2,1,0:T(8,128)S(1)}, s32[]{:T(128)}, s32[]{:T(128)}, s32[65]{0:T(128)S(1)}, /*index=5*/s32[65]{0:T(128)S(1)}, f32[32,8...) while((s32[]{:T(128)}, f32[4,8,256]{2,1,0:T(8,128)S(1)}, ...), condition=%wide.region_19.20_spmd, body=%wide.region_17.19_spmd.sunk | while | flops 14687269 | bytes 213307 | solution.py:71
  344.9 0.8 fusion.172
  349.6 0.8 fusion.172
  358.9 0.8 fusion.172
  377.5 0.8 fusion.172
  382.1 0.8 fusion.172
  386.7 0.8 fusion.172
  391.4 0.8 fusion.172
  396.0 0.8 fusion.172
  400.7 0.8 fusion.172
  412.1 6.3 reduce-scatter.9.cloned.1.call-done
  418.4 0.9 multiply_reduce_fusion.2
  419.3 39.3 %psum.45 = f32[8]{0:T(128)S(1)} all-reduce(f32[8]{0:T(128)S(1)} %multiply_reduce_fusion.2), channel_id=1, replica_groups=mesh['row'=2,'col'=16] {'row','col'}, use_global_device_ids=true, to_apply=%region_22.23 | all-reduce | flops 8 | bytes 64 | tf_op jit(solution)/shard_map/psum | solution.py:81
  458.9 40.9 %psum.46 = f32[8]{0:T(128)S(1)} all-reduce(f32[8]{0:T(128)S(1)} %get-tuple-element.306), channel_id=1, replica_groups=mesh['row'=2,'col'=16] {'row','col'}, use_global_device_ids=true, to_apply=%region_24.25 | all-reduce | flops 8 | bytes 64 | tf_op jit(solution)/shard_map/psum | solution.py:25
  499.9 21.8 %all_gather.23 = f32[32,8,256]{2,1,0:T(8,128)S(1)} all-gather(f32[2,8,256]{2,1,0:T(8,128)S(1)} %multiply_add_fusion.2), channel_id=1, replica_groups=mesh['row'=2,'col'=16] {'col'}, dimensions={0}, use_global_device_ids=true | all-gather | bytes 278528 | tf_op jit(solution)/shard_map/all_gather | solution.py:59
  521.7 69.7 %while.43 = (s32[]{:T(128)}, f32[4,8,256]{2,1,0:T(8,128)S(1)}, s32[]{:T(128)}, s32[]{:T(128)}, s32[65]{0:T(128)S(1)}, /*index=5*/s32[65]{0:T(128)S(1)}, f32[32,8...) while((s32[]{:T(128)}, f32[4,8,256]{2,1,0:T(8,128)S(1)}, ...), condition=%wide.region_27.28_spmd, body=%wide.region_25.27_spmd.sunk | while | flops 14687269 | bytes 213307 | solution.py:71
  548.1 0.8 fusion.177
  552.8 0.8 fusion.177
  576.0 0.8 fusion.177
  585.3 0.8 fusion.177
  589.9 0.8 fusion.177
  592.0 6.4 reduce-scatter.11.cloned.1.call-done
  598.4 0.9 multiply_reduce_fusion
  599.3 39.3 %psum.47 = f32[8]{0:T(128)S(1)} all-reduce(f32[8]{0:T(128)S(1)} %multiply_reduce_fusion), channel_id=1, replica_groups=mesh['row'=2,'col'=16] {'row','col'}, use_global_device_ids=true, to_apply=%region_30.31 | all-reduce | flops 8 | bytes 64 | tf_op jit(solution)/shard_map/psum | solution.py:81
  (1109 shorter events, 221.3 us)
Async XLA Ops:
  7.2 131.8 %reduce-scatter.5.cloned.1.call-start = ((), (), s32[]{:S(2)}) async-start(), calls=%async_computation.4 | async-start | bytes 49152 | tf_op jit(solution)/shard_map/reduce_scatter | solution.py:72
  12.8 0.7 copy-start.10
  41.3 0.8 copy-start.5
  129.6 0.6 copy-start.1
  129.6 9.4 %copy-start.6 = (f32[2,256]{1,0:T(2,128)S(1)}, f32[2,256]{1,0:T(2,128)}, u32[]{:S(2)}) copy-start(f32[2,256]{1,0:T(2,128)} %param.14) | copy-start | bytes 6148
  129.6 9.4 %copy-start.9 = (f32[2,8,256]{2,1,0:T(8,128)S(1)}, f32[2,8,256]{2,1,0:T(8,128)}, u32[]{:S(2)}) copy-start(f32[2,8,256]{2,1,0:T(8,128)} %param.15) | copy-start | bytes 49156
  130.2 108.2 %reduce-scatter.7.cloned.1.call-start = ((), (), s32[]{:S(2)}) async-start(), calls=%async_computation.5 | async-start | bytes 49152 | tf_op jit(solution)/shard_map/reduce_scatter | solution.py:72
  231.4 0.6 copy-start.2
  232.0 186.4 %reduce-scatter.9.cloned.1.call-start = ((), (), s32[]{:S(2)}) async-start(), calls=%async_computation.6 | async-start | bytes 49152 | tf_op jit(solution)/shard_map/reduce_scatter | solution.py:72
  238.4 40.3 %copy-start.4 = (f32[2,8,256]{2,1,0:T(8,128)S(1)}, f32[2,8,256]{2,1,0:T(8,128)}, u32[]{:S(2)}) copy-start(f32[2,8,256]{2,1,0:T(8,128)} %reduce-scatter.7.cloned.1.call-done) | copy-start | bytes 49156
  411.4 0.6 copy-start.3
  412.0 186.4 %reduce-scatter.11.cloned.1.call-start = ((), (), s32[]{:S(2)}) async-start(), calls=%async_computation.7 | async-start | bytes 49152 | tf_op jit(solution)/shard_map/reduce_scatter | solution.py:72
  418.4 40.2 %copy-start.8 = (f32[2,8,256]{2,1,0:T(8,128)S(1)}, f32[2,8,256]{2,1,0:T(8,128)}, u32[]{:S(2)}) copy-start(f32[2,8,256]{2,1,0:T(8,128)} %reduce-scatter.9.cloned.1.call-done) | copy-start | bytes 49156
  591.4 0.6 copy-start
  598.4 40.2 %copy-start.7 = (f32[2,8,256]{2,1,0:T(8,128)S(1)}, f32[2,8,256]{2,1,0:T(8,128)}, u32[]{:S(2)}) copy-start(f32[2,8,256]{2,1,0:T(8,128)} %reduce-scatter.11.cloned.1.call-done) | copy-start | bytes 49156
Sparse Core Ops, SparseCore 0:
  130.3 8.6 reduce-scatter.4
  232.2 6.2 reduce-scatter.6
  412.2 6.2 reduce-scatter.8
  592.1 6.2 reduce-scatter.10
where the time goes:
time: 649 us; the launch traced here: 646 us
  blocking collectives  311 us (48%)
  local copies, waits for them, and re-layouts  108 us (17%)
  other arithmetic  88.9 us (14%)
  matrix products  49 us (8%)
  loops' own time  45.2 us (7%)
  waiting for transfers between devices  27.9 us (4%)
  between operations  15.2 us (2%)
    psum x3, blocking collectives, squares(): return lax.psum(jnp.sum(residual * residual, axis=(0, 2)), ('row', 'col'))  121 us
    all_gather x4, blocking collectives, apply_operator(): pieces = lax.all_gather(vectors, 'col', axis=0, tiled=True)  83.5 us
    psum x2, blocking collectives, shards(): lax.psum(jnp.sum(direction * applied, axis=(0, 2)), ('row', 'col'))  78.6 us
    dot_general x60, matrix products, visit(): jnp.einsum('pab,psa->psb', weights, pieces[local_rows], precision=lax.Pre...  49 us
    another operation x4, loops' own time, apply_operator(): gathered_sum = lax.fori_loop(0, turns, visit, empty)  45.2 us
    convert_element_type x60, other arithmetic, group_weights(): inside = (indices < last).astype(jnp.float32)  38.1 us
    scatter-add x60, other arithmetic, visit(): return running.at[cols_group].add(product)  36.6 us
    gather x60, local copies, waits for them, and re-layouts, group_weights(): col_points[cols_group]  34.3 us
  transfers between devices with their start and end apart: 4, of which 4 were waited for; matrix products, arithmetic and copies ran while one was open for 0% of the time, Pallas kernels for 0%

commit v1 on v0

v1 whole, which is shorter than its diff:
```python
import functools

import jax
import jax.numpy as jnp
from jax import lax
from jax.experimental import pallas as pl
from jax.experimental.pallas import tpu as pltpu
from jax.sharding import PartitionSpec as P

ITERS = 3
GROUP = 4
NEAR = 27
CAPACITY = -(-NEAR // GROUP) * GROUP
CORES = 2
MESH = pl.DeviceIdType.MESH
VMEM_SPEC = pl.BlockSpec(memory_space=pltpu.VMEM)
SMEM_SPEC = pl.BlockSpec(memory_space=pltpu.SMEM)
ANY_SPEC = pl.BlockSpec(memory_space=pl.ANY)


def factors(mesh_shape):
    rows, cols = mesh_shape
    chips = cols // CORES
    wide = 1
    while wide * wide * 4 <= chips:
        wide *= 2
    return rows, chips // wide, wide, CORES


def gather_kernel(dims, count, *refs):
    xs, zs, ys, cs = dims
    ins, outs = refs[:count], refs[count : 2 * count]
    send_sem, recv_sem, local_sem = refs[2 * count :]
    x = lax.axis_index("row")
    col = lax.axis_index("col")
    z, y, c = col // (ys * cs), (col // cs) % ys, col % cs

    def device(xx, zz, yy, cc):
        return (xx, (zz * ys + yy) * cs + cc)

    def slot(xx, zz, yy, cc):
        return ((xx * zs + zz) * ys + yy) * cs + cc

    balanced = xs == 2 and ys == 2
    partners = [device(x, (z + k) % zs, y, c) for k in range(1, zs)]
    partners += [device(x, z, (y + k) % ys, c) for k in range(1, ys)]
    partners += [device((x + k) % xs, z, y, c) for k in range(1, xs)]
    partners += [device(x, z, y, 1 - c)]
    barrier = pltpu.get_barrier_semaphore()
    for partner in partners:
        pl.semaphore_signal(barrier, inc=1, device_id=partner, device_id_type=MESH)
    local = []
    for a in range(count):
        copy = pltpu.make_async_copy(ins[a], outs[a].at[slot(x, z, y, c)], local_sem.at[a])
        copy.start()
        local.append(copy)
    pl.semaphore_wait(barrier, len(partners))

    numbers = iter(range(10**6))
    sent = []

    def send(a, source, place, target):
        number = next(numbers)
        copy = pltpu.make_async_remote_copy(
            src_ref=source,
            dst_ref=outs[a].at[place],
            send_sem=send_sem.at[number],
            recv_sem=recv_sem.at[number],
            device_id=target,
            device_id_type=MESH,
        )
        copy.start()
        sent.append(copy)
        return copy

    mine = slot(x, z, y, c)
    other = device(x, z, y, 1 - c)
    along_z = {}
    for k in range(1, zs):
        for a in range(count):
            along_z[k, a] = send(a, ins[a], mine, device(x, (z + k) % zs, y, c))
    for a in range(count):
        local[a].wait()

    if xs == 2 and ys == 2:
        x2, y2 = (x + c) % 2, (y + 1 - c) % 2
        x3, y3 = (x + 1 - c) % 2, (y + c) % 2
        ahead, aside, late, swaps = {}, {}, {}, []
        steps = [(k, a) for k in range(zs) for a in range(count)]
        for k, a in steps:
            if k:
                along_z[k, a].wait_recv()
            place = slot(x, (z - k + zs) % zs, y, c)
            ahead[k, a] = send(a, outs[a].at[place], place, device(x2, z, y2, c))
            aside[k, a] = send(a, outs[a].at[place], place, device(x3, z, y3, c))
            swaps.append(send(a, outs[a].at[place], place, other))
        for k, a in steps:
            ahead[k, a].wait_recv()
            place = slot(x2, (z - k + zs) % zs, y2, c)
            late[k, a] = send(a, outs[a].at[place], place, device(x3, z, y3, c))
            swaps.append(send(a, outs[a].at[place], place, other))
        for k, a in steps:
            aside[k, a].wait_recv()
            place = slot(x3, (z - k + zs) % zs, y3, c)
            swaps.append(send(a, outs[a].at[place], place, other))
        for k, a in steps:
            late[k, a].wait_recv()
            place = slot(1 - x, (z - k + zs) % zs, 1 - y, c)
            swaps.append(send(a, outs[a].at[place], place, other))
        for copy in swaps:
            copy.wait_recv()
        for copy in sent:
            copy.wait_send()
        return

    def across(places, targets):
        for place in places:
            for a in range(count):
                for target in targets:
                    send(a, outs[a].at[place], place, target)

    def settle():
        for copy in sent:
            copy.wait()
        del sent[:]

    settle()
    across(
        [slot(x, zz, y, c) for zz in range(zs)],
        [device(x, z, (y + k) % ys, c) for k in range(1, ys)],
    )
    settle()
    across(
        [slot(x, zz, yy, c) for zz in range(zs) for yy in range(ys)],
        [device((x + k) % xs, z, y, c) for k in range(1, xs)],
    )
    settle()
    across(
        [slot(xx, zz, yy, c) for xx in range(xs) for zz in range(zs) for yy in range(ys)],
        [other],
    )
    settle()


def all_gather(dims, collective_id, *slabs):
    xs, zs, ys, cs = dims
    devices = xs * zs * ys * cs
    count = len(slabs)
    copies = count * (devices - 1)
    return pl.pallas_call(
        functools.partial(gather_kernel, dims, count),
        out_shape=[jax.ShapeDtypeStruct((devices,) + s.shape, s.dtype) for s in slabs],
        in_specs=[VMEM_SPEC] * count,
        out_specs=[VMEM_SPEC] * count,
        scratch_shapes=[
            pltpu.SemaphoreType.DMA((copies,)),
            pltpu.SemaphoreType.DMA((copies,)),
            pltpu.SemaphoreType.DMA((count,)),
        ],
        compiler_params=pltpu.CompilerParams(collective_id=collective_id, has_side_effects=True),
    )(*slabs)


def split_rows(values):
    high = values.astype(jnp.bfloat16)
    low = (values - high.astype(jnp.float32)).astype(jnp.bfloat16)
    return jnp.concatenate([high, low], axis=0)


def product(near_ref, groups, vectors_ref, blocks, place, tile, wait):
    depth = 2 * tile * GROUP

    def step(g, total):
        wait(g)
        parts = []
        for i in range(GROUP):
            part = vectors_ref[near_ref[place, g * GROUP + i]]
            parts += [part, part]
        first = pl.multiple_of((place * (CAPACITY // GROUP) + g) * depth, depth)
        return total + jnp.dot(
            jnp.concatenate(parts, axis=1),
            blocks[pl.ds(first, depth), :],
            preferred_element_type=jnp.float32,
        )

    rhs2 = vectors_ref.shape[1]
    total = lax.fori_loop(0, groups, step, jnp.zeros((rhs2, tile), jnp.float32))
    return total[: rhs2 // 2] + total[rhs2 // 2 :]


def block_copy(blocks, blocks_hbm, sems, place, g, depth, out):
    number = place * (CAPACITY // GROUP) + g
    part = pl.ds(pl.multiple_of(number * depth, depth), depth)
    if out:
        return pltpu.make_async_copy(blocks.at[part, :], blocks_hbm.at[part, :], sems.at[number])
    return pltpu.make_async_copy(blocks_hbm.at[part, :], blocks.at[part, :], sems.at[number])


def build_kernel(
    flags_ref, points_ref, own_ref, guess_ref, own_guess_ref, side_ref, noise_ref,
    residual_ref, blocks_hbm, near_ref, count_ref, blocks, vectors_ref, sems,
):
    tiles, tile = points_ref.shape[0], points_ref.shape[2]
    own = own_ref.shape[0]
    depth = 2 * tile * GROUP
    rows = 32

    def split_one(t, carry):
        vectors_ref[t] = split_rows(guess_ref[t])
        return carry

    lax.fori_loop(0, tiles, split_one, 0, unroll=4)
    for place in range(own):
        def listing(t, number):
            near_ref[place, number] = t
            return number + flags_ref[place, t]

        number = lax.fori_loop(0, tiles, listing, jnp.int32(0))
        for i in range(GROUP):
            near_ref[place, number + i] = 0
        groups = (number + GROUP - 1) // GROUP
        count_ref[place] = groups
        right = own_ref[place]
        base = place * CAPACITY * 2 * tile

        def one(e, carry):
            left = points_ref[near_ref[place, e]].T
            start = base + e * (2 * tile)
            for chunk in range(tile // rows):
                squared = None
                for component in range(3):
                    spacing = (
                        left[chunk * rows : (chunk + 1) * rows, component : component + 1]
                        - right[component : component + 1, :]
                    )
                    term = spacing * spacing
                    squared = term if squared is None else squared + term
                distance = jnp.sqrt(squared)
                remain = jnp.maximum(1.0 - distance, 0.0)
                remain = remain * remain
                weights = remain * remain * (4.0 * distance + 1.0)
                high = weights.astype(jnp.bfloat16)
                low = (weights - high.astype(jnp.float32)).astype(jnp.bfloat16)
                at = pl.multiple_of(start + chunk * rows, rows)
                blocks[pl.ds(at, rows), :] = high
                at = pl.multiple_of(start + tile + chunk * rows, rows)
                blocks[pl.ds(at, rows), :] = low
            return carry

        def empty(e, carry):
            at = pl.multiple_of(base + e * (2 * tile), 2 * tile)
            blocks[pl.ds(at, 2 * tile), :] = jnp.zeros((2 * tile, tile), jnp.bfloat16)
            return carry

        lax.fori_loop(0, number, one, 0)
        lax.fori_loop(number, groups * GROUP, empty, 0)

        def start_out(g, carry):
            block_copy(blocks, blocks_hbm, sems, place, g, depth, True).start()
            return carry

        lax.fori_loop(0, groups, start_out, 0)
        image = product(near_ref, groups, vectors_ref, blocks, place, tile, lambda g: None)
        image = image + noise_ref[place : place + 1, :] * own_guess_ref[place]
        residual_ref[place] = side_ref[place] - image
    for place in range(own):
        def wait_out(g, carry):
            block_copy(blocks, blocks_hbm, sems, place, g, depth, True).wait()
            return carry

        lax.fori_loop(0, count_ref[place], wait_out, 0)


def step_kernel(first, *refs):
    refs = list(refs)
    near_ref, count_ref, me_ref, noise_ref, blocks_hbm = refs[:5]
    refs = refs[5:]
    if first:
        (res_ref, field_ref), refs = refs[:2], refs[2:]
    else:
        (image_ref, res_ref, dir_ref, norm_ref, field_ref), refs = refs[:5], refs[5:]
    (out_image, out_res, out_dir, out_norm, out_field, out_dot), refs = refs[:6], refs[6:]
    blocks, vectors_ref, sems = refs
    tiles, rhs, tile = res_ref.shape
    own = noise_ref.shape[0]
    depth = 2 * tile * GROUP
    me = me_ref[0]
    for place in range(own):
        def start_in(g, carry):
            block_copy(blocks, blocks_hbm, sems, place, g, depth, False).start()
            return carry

        lax.fori_loop(0, count_ref[place], start_in, 0)
    zero = jnp.zeros((rhs, tile), jnp.float32)
    if first:
        def square(t, total):
            value = res_ref[t]
            vectors_ref[t] = split_rows(value)
            out_dir[t] = value
            out_res[t] = value
            return total + value * value

        norm = jnp.sum(lax.fori_loop(0, tiles, square, zero, unroll=4), axis=1, keepdims=True)
        out_field[...] = field_ref[...]
    else:
        def dots(t, total):
            return total + dir_ref[t] * image_ref[t]

        norm_old = norm_ref[:, :1]
        inner = jnp.sum(lax.fori_loop(0, tiles, dots, zero, unroll=4), axis=1, keepdims=True)
        step_size = norm_old / inner
        for place in range(own):
            out_field[place] = field_ref[place] + step_size * dir_ref[me * own + place]

        def descend(t, total):
            value = res_ref[t] - step_size * image_ref[t]
            out_res[t] = value
            return total + value * value

        norm = jnp.sum(lax.fori_loop(0, tiles, descend, zero, unroll=4), axis=1, keepdims=True)
        turn = norm / norm_old

        def redirect(t, carry):
            value = out_res[t] + turn * dir_ref[t]
            out_dir[t] = value
            vectors_ref[t] = split_rows(value)
            return carry

        lax.fori_loop(0, tiles, redirect, 0, unroll=4)
    out_norm[...] = jnp.broadcast_to(norm, out_norm.shape)
    total = zero
    for place in range(own):
        groups = count_ref[place]

        def wait(g):
            block_copy(blocks, blocks_hbm, sems, place, g, depth, False).wait()

        image = product(near_ref, groups, vectors_ref, blocks, place, tile, wait)
        value = out_dir[me * own + place]
        image = image + noise_ref[place : place + 1, :] * value
        out_image[place] = image
        total = total + value * image
    out_dot[...] = jnp.broadcast_to(jnp.sum(total, axis=1, keepdims=True), out_dot.shape)


def shards(mesh_shape, coords, noise_var, right_side, start_guess, tile_pairs):
    dims = factors(mesh_shape)
    devices = mesh_shape[0] * mesh_shape[1]
    own, _, tile = coords.shape
    rhs = right_side.shape[1]
    tiles = own * devices
    me = (lax.axis_index("row") * mesh_shape[1] + lax.axis_index("col")).astype(jnp.int32)
    padded = jnp.pad(coords, ((0, 0), (0, 5), (0, 0)))
    points, guess = all_gather(dims, 0, padded, start_guess)
    points = points.reshape(tiles, 8, tile)
    guess = guess.reshape(tiles, rhs, tile)
    low, high = jnp.min(points, axis=2), jnp.max(points, axis=2)
    own_low, own_high = jnp.min(padded, axis=2), jnp.max(padded, axis=2)
    gap = jnp.maximum(low[None] - own_high[:, None], own_low[:, None] - high[None])
    flags = jnp.all(gap < 1.0, axis=2).astype(jnp.int32)

    f32 = jnp.float32
    full = jax.ShapeDtypeStruct((tiles, rhs, tile), f32)
    slab = jax.ShapeDtypeStruct((own, rhs, tile), f32)
    small = jax.ShapeDtypeStruct((rhs, 128), f32)
    block_shape = (own * CAPACITY * 2 * tile, tile)
    scratch = [
        pltpu.VMEM(block_shape, jnp.bfloat16),
        pltpu.VMEM((tiles, 2 * rhs, tile), jnp.bfloat16),
        pltpu.SemaphoreType.DMA((own * CAPACITY // GROUP,)),
    ]
    params = pltpu.CompilerParams(vmem_limit_bytes=56 * 2**20)
    residual, blocks, near, count = pl.pallas_call(
        build_kernel,
        out_shape=[
            slab,
            jax.ShapeDtypeStruct(block_shape, jnp.bfloat16),
            jax.ShapeDtypeStruct((own, CAPACITY + GROUP), jnp.int32),
            jax.ShapeDtypeStruct((own,), jnp.int32),
        ],
        in_specs=[SMEM_SPEC] + [VMEM_SPEC] * 6,
        out_specs=[VMEM_SPEC, ANY_SPEC, SMEM_SPEC, SMEM_SPEC],
        scratch_shapes=scratch,
        compiler_params=params,
    )(flags, points, padded, guess, start_guess, right_side, noise_var)

    def advance(first, operands):
        return pl.pallas_call(
            functools.partial(step_kernel, first),
            out_shape=[slab, full, full, small, slab, small],
            in_specs=[SMEM_SPEC] * 3 + [VMEM_SPEC, ANY_SPEC] + [VMEM_SPEC] * len(operands),
            out_specs=[VMEM_SPEC] * 6,
            scratch_shapes=scratch,
            compiler_params=params,
        )(near, count, me[None], noise_var, blocks, *operands)

    (gathered,) = all_gather(dims, 1, residual)
    image, residual, direction, norm, field, dot = advance(
        True, (gathered.reshape(full.shape), start_guess)
    )
    for iteration in range(1, ITERS):
        (gathered,) = all_gather(dims, 1 + iteration, image)
        image, residual, direction, norm, field, dot = advance(
            False, (gathered.reshape(full.shape), residual, direction, norm, field)
        )
    (dots,) = all_gather(dims, 1 + ITERS, dot)
    step_size = (norm[:, :1] / jnp.sum(dots[:, :, :1], axis=0))[None]
    own_res = lax.dynamic_slice_in_dim(residual, me * own, own)
    own_dir = lax.dynamic_slice_in_dim(direction, me * own, own)
    return field + step_size * own_dir, own_res - step_size * image


def solution(mesh):
    placed = (
        P(("row", "col"), None, None),
        P(("row", "col"), None),
        P(("row", "col"), None, None),
        P(("row", "col"), None, None),
        P("row", "col", None, None),
    )
    return jax.shard_map(
        functools.partial(shards, (mesh.shape["row"], mesh.shape["col"])),
        mesh=mesh,
        in_specs=placed,
        out_specs=(P(("row", "col"), None, None), P(("row", "col"), None, None)),
        check_vma=False,
    )
```

time: 649 us -> 121 us (0.19)
  blocking collectives: 311 us -> 0 us
  Pallas kernels: 0 us -> 112 us
  local copies, waits for them, and re-layouts: 108 us -> 0.9 us
  other arithmetic: 88.9 us -> 5.87 us
  matrix products: 49 us -> 0 us
  loops' own time: 45.2 us -> 0 us
  waiting for transfers between devices: 27.9 us -> 0 us
  between operations: 15.2 us -> 0.73 us
    psum x5 -> x0, blocking collectives: 200 us -> none  [the longest x3 121 us: squares(): return lax.psum(jnp.sum(residual * residual, axis=(0, 2)), ('row', 'col'))]
    pallas_call x0 -> x9, Pallas kernels: none -> 112 us  [the longest x5 75.5 us: all_gather(): pl.pallas_call(functools.partial(gather_kernel, dims, count), out_shape=[...]
    all_gather x6 -> x0, blocking collectives: 111 us -> none  [the longest x4 83.5 us: apply_operator(): pieces = lax.all_gather(vectors, 'col', axis=0, tiled=True)]
    gather x182 -> x0, local copies, waits for them, and re-layouts: 103 us -> none  [the longest x60 34.3 us: group_weights(): col_points[cols_group]]
    dot_general x60 -> x0, matrix products: 49 us -> none  [visit(): jnp.einsum('pab,psa->psb', weights, pieces[local_rows], precision=lax.Pre...]
    another operation x4 -> x0, loops' own time: 45.2 us -> none  [apply_operator(): gathered_sum = lax.fori_loop(0, turns, visit, empty)]
    convert_element_type x60 -> x1, other arithmetic: 38.1 us -> 0.55 us  [shards(): flags = jnp.all(gap < 1.0, axis=2).astype(jnp.int32)]
    scatter-add x60 -> x0, other arithmetic: 36.6 us -> none  [visit(): return running.at[cols_group].add(product)]
  transfers between devices with their start and end apart: 4 -> 0, of which waited for: 4 -> 0; matrix products, arithmetic and copies ran while one was open for 0% -> 0% of each run, Pallas kernels for 0% -> 0%
where the time goes in v1:
time: 121 us; the launch traced here: 120 us
  Pallas kernels  112 us (93%)
  other arithmetic  5.87 us (5%)
    pallas_call x5, Pallas kernels, all_gather(): pl.pallas_call(functools.partial(gather_kernel, dims, count), out_shape=[...  75.5 us
    pallas_call x3, Pallas kernels, advance(): pl.pallas_call(functools.partial(step_kernel, first), out_shape=[slab, fu...  18.9 us
    pallas_call x1, Pallas kernels, shards(): pl.pallas_call(build_kernel, out_shape=[slab, jax.ShapeDtypeStruct(block_...  18.1 us

profile of v1, /device:TPU:0, one launch (start us, length us, event | category | flops | bytes accessed | tf_op | source)
XLA Modules:
  0.0 119.9 jit_solution(16864352433059415642)
XLA Ops:
  0.6 0.7 copy.12
  1.3 0.6 pad_reduce_fusion.1
  1.9 19.6 %shard_map.59 = (f32[32,2,8,256]{3,2,1,0:T(8,128)}, f32[32,2,8,256]{3,2,1,0:T(8,128)}) custom-call(f32[2,8,256]{2,1,0:T(8,128)} %get-tuple-element.50.refs_0_.own_ref, f32[2,8,256]{2,1,0:T(8,128)} %refs_6_.1), custom_call_target="tpu_custom_call" | custom-call | tf_op jit(solution)/shard_map/pallas_call | solution.py:150
  21.6 1.3 %fusion.1 = (f32[32,2,8]{2,1,0:T(2,128)S(1)}, f32[32,2,8]{2,1,0:T(2,128)S(1)}) fusion(f32[32,2,8,256]{3,2,1,0:T(8,128)} %get-tuple-element.24), kind=kLoop, calls=%fused_computation.8 | loop fusion | flops 261120 | bytes 528384 | tf_op jit(solution)/shard_map/reduce_min | solution.py:357
  22.9 0.1 copy.13
  22.9 0.1 copy.14
  23.0 0.1 fusion
  23.1 0.6 convert_element_type.5.flags_ref
  23.7 18.1 %shard_map.60 = (f32[2,8,256]{2,1,0:T(8,128)}, bf16[28672,256]{1,0:T(8,128)(2,1)}, s32[2,32]{1,0:T(2,128)}, s32[2]{0:T(128)}) custom-call(s32[2,64]{1,0:T(2,128)} %convert_element_type.5.flags_ref, f32[64,8,256]{2,1,0:T(8,128)} %bitcast.10, f32[2,8,256]{2,1,0:T(8,128)} %get-tuple-element.50.refs_0_.own_ref, f32[64,8,256]{2,1,0:T(8,128)} %bitcast.13, ...), custom_call_target="tpu_custom_call" | custom-call | tf_op jit(solution)/shard_map/pallas_call | solution.py:373
  41.7 13.5 %shard_map.61 = f32[32,2,8,256]{3,2,1,0:T(8,128)} custom-call(f32[2,8,256]{2,1,0:T(8,128)} %get-tuple-element.29.refs_0_), custom_call_target="tpu_custom_call" | custom-call | tf_op jit(solution)/shard_map/pallas_call | solution.py:150
  55.2 5.9 %shard_map.62 = (f32[2,8,256]{2,1,0:T(8,128)}, f32[64,8,256]{2,1,0:T(8,128)}, f32[64,8,256]{2,1,0:T(8,128)}, f32[8,128]{1,0:T(8,128)}, f32[2,8,256]{2,1,0:T(8,128)}, /*index=5*/f32[8,128]{1,0:T(8,128)}) custom-call(s32[2,32]{1,0:T(2,128)} %get-tuple-element.26.refs_0_, s32[2]{0:T(128)} %get-tuple-element.27.refs_1_, s32[1]{0:T(128)} %bitcast.4.refs_2_, ...), custom_call_target="tpu_custom_call" | custom-call | tf_op jit(solution)/shard_map/pallas_call | solution.py:388
  61.1 14.9 %shard_map.63 = f32[32,2,8,256]{3,2,1,0:T(8,128)} custom-call(f32[2,8,256]{2,1,0:T(8,128)} %get-tuple-element.30.refs_0_), custom_call_target="tpu_custom_call" | custom-call | tf_op jit(solution)/shard_map/pallas_call | solution.py:150
  76.0 6.5 %shard_map.64 = (f32[2,8,256]{2,1,0:T(8,128)}, f32[64,8,256]{2,1,0:T(8,128)}, f32[64,8,256]{2,1,0:T(8,128)}, f32[8,128]{1,0:T(8,128)}, f32[2,8,256]{2,1,0:T(8,128)}, /*index=5*/f32[8,128]{1,0:T(8,128)}) custom-call(s32[2,32]{1,0:T(2,128)} %get-tuple-element.26.refs_0_, s32[2]{0:T(128)} %get-tuple-element.27.refs_1_, s32[1]{0:T(128)} %bitcast.4.refs_2_, ...), custom_call_target="tpu_custom_call" | custom-call | tf_op jit(solution)/shard_map/pallas_call | solution.py:388
  82.5 13.1 %shard_map.65 = f32[32,2,8,256]{3,2,1,0:T(8,128)} custom-call(f32[2,8,256]{2,1,0:T(8,128)} %get-tuple-element.35.refs_0_), custom_call_target="tpu_custom_call" | custom-call | tf_op jit(solution)/shard_map/pallas_call | solution.py:150
  95.6 6.5 %shard_map.66 = (f32[2,8,256]{2,1,0:T(8,128)}, f32[64,8,256]{2,1,0:T(8,128)}, f32[64,8,256]{2,1,0:T(8,128)}, f32[8,128]{1,0:T(8,128)}, f32[2,8,256]{2,1,0:T(8,128)}, /*index=5*/f32[8,128]{1,0:T(8,128)}) custom-call(s32[2,32]{1,0:T(2,128)} %get-tuple-element.26.refs_0_, s32[2]{0:T(128)} %get-tuple-element.27.refs_1_, s32[1]{0:T(128)} %bitcast.4.refs_2_, ...), custom_call_target="tpu_custom_call" | custom-call | tf_op jit(solution)/shard_map/pallas_call | solution.py:388
  102.1 14.4 %shard_map.67 = f32[32,8,128]{2,1,0:T(8,128)} custom-call(f32[8,128]{1,0:T(8,128)} %get-tuple-element.42.refs_0_), custom_call_target="tpu_custom_call" | custom-call | tf_op jit(solution)/shard_map/pallas_call | solution.py:150
  116.5 1.1 slice_reduce_fusion
  117.5 0.1 copy.15
  117.6 0.8 divide_reduce_fusion
  118.4 1.5 %multiply_subtract_fusion = (f32[2,8,256]{2,1,0:T(8,128)}, f32[2,8,256]{2,1,0:T(8,128)}) fusion(f32[2,8,256]{2,1,0:T(8,128)} %get-tuple-element.45, f32[64,8,256]{2,1,0:T(8,128)} %get-tuple-element.44, s32[]{:T(128)S(6)} %select_n.4, f32[8]{0:T(128)S(1)} %divide_reduce_fusion, f32[2,8,256]{2,1,0:T(8,128)} %get-tuple-element.40, ...), kind=kLoop, calls=%fused_computation.1 | loop fusion | flops 16384 | bytes 98340 | tf_op jit(solution)/shard_map/sub | solution.py:410

commit v2 on v0

v2 whole, which is shorter than its diff:
```python
import functools

import jax
import jax.numpy as jnp
from jax import lax
from jax.experimental import pallas as pl
from jax.experimental.pallas import tpu as pltpu
from jax.sharding import PartitionSpec as P

ITERS = 3
GROUP = 4
NEAR = 27
CAPACITY = -(-NEAR // GROUP) * GROUP
CORES = 2
MESH = pl.DeviceIdType.MESH
VMEM_SPEC = pl.BlockSpec(memory_space=pltpu.VMEM)
SMEM_SPEC = pl.BlockSpec(memory_space=pltpu.SMEM)
ANY_SPEC = pl.BlockSpec(memory_space=pl.ANY)


def factors(mesh_shape):
    rows, cols = mesh_shape
    chips = cols // CORES
    wide = 1
    while wide * wide * 4 <= chips:
        wide *= 2
    return rows, chips // wide, wide, CORES


def position(dims):
    xs, zs, ys, cs = dims
    x = lax.axis_index("row")
    col = lax.axis_index("col")
    return x, col // (ys * cs), (col // cs) % ys, col % cs


def gather_partners(dims):
    xs, zs, ys, cs = dims
    x, z, y, c = position(dims)
    partners = [(x, (((z + k) % zs) * ys + y) * cs + c) for k in range(1, zs)]
    partners += [(x, (z * ys + (y + k) % ys) * cs + c) for k in range(1, ys)]
    partners += [((x + k) % xs, (z * ys + y) * cs + c) for k in range(1, xs)]
    partners += [(x, (z * ys + y) * cs + 1 - c)]
    return partners


def gather(dims, ins, outs, send_sem, recv_sem, local_sem):
    xs, zs, ys, cs = dims
    count = len(ins)
    x, z, y, c = position(dims)

    def device(xx, zz, yy, cc):
        return (xx, (zz * ys + yy) * cs + cc)

    def slot(xx, zz, yy, cc):
        return ((xx * zs + zz) * ys + yy) * cs + cc

    local = []
    for a in range(count):
        copy = pltpu.make_async_copy(ins[a], outs[a].at[slot(x, z, y, c)], local_sem.at[a])
        copy.start()
        local.append(copy)

    numbers = iter(range(10**6))
    sent = []

    def send(a, source, place, target):
        number = next(numbers)
        copy = pltpu.make_async_remote_copy(
            src_ref=source,
            dst_ref=outs[a].at[place],
            send_sem=send_sem.at[number],
            recv_sem=recv_sem.at[number],
            device_id=target,
            device_id_type=MESH,
        )
        copy.start()
        sent.append(copy)
        return copy

    mine = slot(x, z, y, c)
    other = device(x, z, y, 1 - c)
    along_z = {}
    for k in range(1, zs):
        for a in range(count):
            along_z[k, a] = send(a, ins[a], mine, device(x, (z + k) % zs, y, c))
    for a in range(count):
        local[a].wait()

    if xs == 2 and ys == 2:
        x2, y2 = (x + c) % 2, (y + 1 - c) % 2
        x3, y3 = (x + 1 - c) % 2, (y + c) % 2
        ahead, aside, late, swaps = {}, {}, {}, []
        steps = [(k, a) for k in range(zs) for a in range(count)]
        for k, a in steps:
            if k:
                along_z[k, a].wait_recv()
            place = slot(x, (z - k + zs) % zs, y, c)
            ahead[k, a] = send(a, outs[a].at[place], place, device(x2, z, y2, c))
            aside[k, a] = send(a, outs[a].at[place], place, device(x3, z, y3, c))
            swaps.append(send(a, outs[a].at[place], place, other))
        for k, a in steps:
            ahead[k, a].wait_recv()
            place = slot(x2, (z - k + zs) % zs, y2, c)
            late[k, a] = send(a, outs[a].at[place], place, device(x3, z, y3, c))
            swaps.append(send(a, outs[a].at[place], place, other))
        for k, a in steps:
            aside[k, a].wait_recv()
            place = slot(x3, (z - k + zs) % zs, y3, c)
            swaps.append(send(a, outs[a].at[place], place, other))
        for k, a in steps:
            late[k, a].wait_recv()
            place = slot(1 - x, (z - k + zs) % zs, 1 - y, c)
            swaps.append(send(a, outs[a].at[place], place, other))
        for copy in swaps:
            copy.wait_recv()
        for copy in sent:
            copy.wait_send()
        return

    def across(places, targets):
        for place in places:
            for a in range(count):
                for target in targets:
                    send(a, outs[a].at[place], place, target)

    def settle():
        for copy in sent:
            copy.wait()
        del sent[:]

    settle()
    across(
        [slot(x, zz, y, c) for zz in range(zs)],
        [device(x, z, (y + k) % ys, c) for k in range(1, ys)],
    )
    settle()
    across(
        [slot(x, zz, yy, c) for zz in range(zs) for yy in range(ys)],
        [device((x + k) % xs, z, y, c) for k in range(1, xs)],
    )
    settle()
    across(
        [slot(xx, zz, yy, c) for xx in range(xs) for zz in range(zs) for yy in range(ys)],
        [other],
    )
    settle()


def gather_kernel(dims, *refs):
    in_ref, out_ref, send_sem, recv_sem, local_sem = refs
    partners = gather_partners(dims)
    barrier = pltpu.get_barrier_semaphore()
    for partner in partners:
        pl.semaphore_signal(barrier, inc=1, device_id=partner, device_id_type=MESH)
    pl.semaphore_wait(barrier, len(partners))
    gather(dims, [in_ref], [out_ref], send_sem, recv_sem, local_sem)


def all_gather(dims, collective_id, slab):
    devices = dims[0] * dims[1] * dims[2] * dims[3]
    return pl.pallas_call(
        functools.partial(gather_kernel, dims),
        out_shape=jax.ShapeDtypeStruct((devices,) + slab.shape, slab.dtype),
        in_specs=[VMEM_SPEC],
        out_specs=VMEM_SPEC,
        scratch_shapes=[
            pltpu.SemaphoreType.DMA((devices - 1,)),
            pltpu.SemaphoreType.DMA((devices - 1,)),
            pltpu.SemaphoreType.DMA((1,)),
        ],
        compiler_params=pltpu.CompilerParams(collective_id=collective_id, has_side_effects=True),
    )(slab)


def split_rows(values):
    high = values.astype(jnp.bfloat16)
    low = (values - high.astype(jnp.float32)).astype(jnp.bfloat16)
    return jnp.concatenate([high, low], axis=0)


def solve_kernel(
    dims, groups,
    near_ref, valid_ref, side_ref, points_ref, own_points_ref, noise_ref, right_ref, guess_ref,
    field_out, residual_out,
    buffers, dir_ref, vectors_ref, blocks, outgoing, dot_ref, dots_ref,
    send_sem, recv_sem, local_sem, dot_send, dot_recv,
):
    cols = dims[1] * dims[2] * dims[3]
    devices = dims[0] * cols
    tiles, tile = points_ref.shape[0], points_ref.shape[2]
    own, rhs, _ = right_ref.shape
    me = lax.axis_index("row") * cols + lax.axis_index("col")

    def peer(k):
        number = (me + k) % devices
        return (number // cols, number % cols)

    barrier = pltpu.get_barrier_semaphore()

    def greet(k, carry):
        pl.semaphore_signal(barrier, inc=1, device_id=peer(k), device_id_type=MESH)
        return carry

    lax.fori_loop(1, devices, greet, 0)
    pl.semaphore_wait(barrier, devices - 1)

    def spread(number, source):
        gather(
            dims, [source], [buffers.at[number]],
            send_sem.at[number], recv_sem.at[number], local_sem.at[number],
        )

    rows = 32
    block = 2 * tile

    def build(e, carry):
        left = points_ref[near_ref[e]].T
        right = own_points_ref[side_ref[e // GROUP]]
        reach = valid_ref[e].astype(jnp.float32)
        for chunk in range(tile // rows):
            squared = None
            for component in range(3):
                spacing = (
                    left[chunk * rows : (chunk + 1) * rows, component : component + 1]
                    - right[component : component + 1, :]
                )
                term = spacing * spacing
                squared = term if squared is None else squared + term
            distance = squared * lax.rsqrt(jnp.maximum(squared, 1e-30))
            remain = jnp.maximum(reach - distance, 0.0)
            remain = remain * remain
            weights = remain * remain * (4.0 * distance + 1.0)
            high = weights.astype(jnp.bfloat16)
            low = (weights - high.astype(jnp.float32)).astype(jnp.bfloat16)
            at = pl.multiple_of(e * block + chunk * rows, rows)
            blocks[pl.ds(at, rows), :] = high
            at = pl.multiple_of(e * block + tile + chunk * rows, rows)
            blocks[pl.ds(at, rows), :] = low
        return carry

    def image_of():
        def step(g, totals):
            parts = []
            for i in range(GROUP):
                part = vectors_ref[near_ref[g * GROUP + i]]
                parts += [part, part]
            first = pl.multiple_of(g * GROUP * block, GROUP * block)
            term = jnp.dot(
                jnp.concatenate(parts, axis=1),
                blocks[pl.ds(first, GROUP * block), :],
                preferred_element_type=jnp.float32,
            )
            place = side_ref[g].astype(jnp.float32)
            return tuple(
                total + term * jnp.maximum(1.0 - jnp.abs(place - float(p)), 0.0)
                for p, total in enumerate(totals)
            )

        start = tuple(jnp.zeros((2 * rhs, tile), jnp.float32) for _ in range(own))
        totals = lax.fori_loop(0, groups, step, start, unroll=2)
        return [total[:rhs] + total[rhs:] for total in totals]

    def over_tiles(body, start):
        def one(i, carry):
            return body(i // own, i % own, carry)

        return lax.fori_loop(0, tiles, one, start, unroll=8)

    zero = jnp.zeros((rhs, tile), jnp.float32)
    noise = [noise_ref[p : p + 1, :] for p in range(own)]

    lax.fori_loop(0, groups * GROUP, build, 0)
    spread(0, guess_ref)

    def take_guess(i, p, carry):
        vectors_ref[i * own + p] = split_rows(buffers[0, i, p])
        return carry

    over_tiles(take_guess, 0)
    for p, image in enumerate(image_of()):
        outgoing[0, p] = right_ref[p] - (image + noise[p] * guess_ref[p])
    spread(1, outgoing.at[0])

    def take_residual(i, p, total):
        value = buffers[1, i, p]
        dir_ref[i, p] = value
        vectors_ref[i * own + p] = split_rows(value)
        return total + value * value

    norm = jnp.sum(over_tiles(take_residual, zero), axis=1, keepdims=True)
    for p in range(own):
        field_out[p] = guess_ref[p]
    for iteration in range(1, ITERS):
        for p, image in enumerate(image_of()):
            outgoing[iteration, p] = image + noise[p] * dir_ref[me, p]
        spread(1 + iteration, outgoing.at[iteration])

        def dots(i, p, total):
            return total + dir_ref[i, p] * buffers[1 + iteration, i, p]

        inner = jnp.sum(over_tiles(dots, zero), axis=1, keepdims=True)
        step_size = norm / inner
        for p in range(own):
            field_out[p] = field_out[p] + step_size * dir_ref[me, p]

        def descend(i, p, total):
            value = buffers[1, i, p] - step_size * buffers[1 + iteration, i, p]
            buffers[1, i, p] = value
            return total + value * value

        norm_next = jnp.sum(over_tiles(descend, zero), axis=1, keepdims=True)
        turn = norm_next / norm

        def redirect(i, p, carry):
            value = buffers[1, i, p] + turn * dir_ref[i, p]
            dir_ref[i, p] = value
            vectors_ref[i * own + p] = split_rows(value)
            return carry

        over_tiles(redirect, 0)
        norm = norm_next

    images, total = [], zero
    for p, image in enumerate(image_of()):
        value = dir_ref[me, p]
        image = image + noise[p] * value
        images.append(image)
        total = total + value * image
    eye = lax.broadcasted_iota(jnp.int32, (rhs, 128), 0) == lax.broadcasted_iota(
        jnp.int32, (rhs, 128), 1
    )
    share = jnp.sum(total, axis=1, keepdims=True)
    row = jnp.sum(jnp.where(eye, share, 0.0), axis=0, keepdims=True)
    dot_ref[...] = row
    dots_ref[me] = row

    def dot_copy(k):
        return pltpu.make_async_remote_copy(
            src_ref=dot_ref,
            dst_ref=dots_ref.at[me],
            send_sem=dot_send.at[k],
            recv_sem=dot_recv.at[k],
            device_id=peer(k),
            device_id_type=MESH,
        )

    def start_dot(k, carry):
        dot_copy(k).start()
        return carry

    def wait_dot(k, carry):
        dot_copy(k).wait()
        return carry

    lax.fori_loop(1, devices, start_dot, 0)
    lax.fori_loop(1, devices, wait_dot, 0)
    inner = jnp.sum(dots_ref[...], axis=0)
    inner = jnp.sum(jnp.where(eye, inner, 0.0), axis=1, keepdims=True)
    step_size = norm / inner
    for p in range(own):
        field_out[p] = field_out[p] + step_size * dir_ref[me, p]
        residual_out[p] = buffers[1, me, p] - step_size * images[p]


def solve(dims, groups, collective_id, *operands):
    devices = dims[0] * dims[1] * dims[2] * dims[3]
    points, right = operands[3], operands[6]
    tiles, tile = points.shape[0], points.shape[2]
    own, rhs, _ = right.shape
    dma = pltpu.SemaphoreType.DMA
    phases = 1 + ITERS
    return pl.pallas_call(
        functools.partial(solve_kernel, dims, groups),
        out_shape=[jax.ShapeDtypeStruct(right.shape, jnp.float32)] * 2,
        in_specs=[SMEM_SPEC] * 3 + [VMEM_SPEC] * 5,
        out_specs=[VMEM_SPEC] * 2,
        scratch_shapes=[
            pltpu.VMEM((phases, devices, own, rhs, tile), jnp.float32),
            pltpu.VMEM((devices, own, rhs, tile), jnp.float32),
            pltpu.VMEM((tiles, 2 * rhs, tile), jnp.bfloat16),
            pltpu.VMEM((groups * GROUP * 2 * tile, tile), jnp.bfloat16),
            pltpu.VMEM((ITERS, own, rhs, tile), jnp.float32),
            pltpu.VMEM((1, 128), jnp.float32),
            pltpu.VMEM((devices, 1, 128), jnp.float32),
            dma((phases, devices - 1)),
            dma((phases, devices - 1)),
            dma((phases, 1)),
            dma((devices,)),
            dma((devices,)),
        ],
        compiler_params=pltpu.CompilerParams(
            collective_id=collective_id, has_side_effects=True, vmem_limit_bytes=60 * 2**20
        ),
    )(*operands)


def shards(mesh_shape, coords, noise_var, right_side, start_guess, tile_pairs):
    dims = factors(mesh_shape)
    devices = mesh_shape[0] * mesh_shape[1]
    own, _, tile = coords.shape
    tiles = own * devices
    me = lax.axis_index("row") * mesh_shape[1] + lax.axis_index("col")
    padded = jnp.pad(coords, ((0, 0), (0, 5), (0, 0)))
    points = all_gather(dims, 0, padded).reshape(tiles, 8, tile)

    low, high = jnp.min(points, axis=2), jnp.max(points, axis=2)
    gap = jnp.maximum(low[None] - high[:, None], low[:, None] - high[None])
    near = jnp.all(gap < 1.0, axis=2).astype(jnp.int32)
    needed = -(-jnp.sum(near, axis=1) // GROUP)
    largest = jnp.max(jnp.sum(needed.reshape(devices, own), axis=1))
    own_near = lax.dynamic_slice_in_dim(near, me * own, own)
    own_needed = lax.dynamic_slice_in_dim(needed, me * own, own)
    ids = jnp.arange(tiles, dtype=jnp.int32)
    rank = jnp.sum(own_near[:, None, :] * (ids[None, None, :] < ids[None, :, None]), axis=2)
    places = jnp.arange(own, dtype=jnp.int32)
    first = jnp.sum(own_needed[None, :] * (places[None, :] < places[:, None]), axis=1)
    goal = jnp.where(own_near > 0, rank + first[:, None] * GROUP, -1)
    capacity = own * CAPACITY
    slots = jnp.arange(capacity, dtype=jnp.int32)
    hit = goal[None] == slots[:, None, None]
    near_ids = jnp.sum(jnp.where(hit, ids[None, None, :], 0), axis=(1, 2)).astype(jnp.int32)
    valid = jnp.sum(hit, axis=(1, 2)).astype(jnp.int32)
    group_ids = jnp.arange(capacity // GROUP, dtype=jnp.int32)
    side = jnp.sum(group_ids[:, None] >= first[None, 1:], axis=1).astype(jnp.int32)

    operands = (near_ids, valid, side, points, padded, noise_var, right_side, start_guess)
    small = own * 4
    return tuple(
        lax.cond(
            largest <= small,
            functools.partial(solve, dims, small, 1),
            functools.partial(solve, dims, capacity // GROUP, 2),
            *operands,
        )
    )


def solution(mesh):
    placed = (
        P(("row", "col"), None, None),
        P(("row", "col"), None),
        P(("row", "col"), None, None),
        P(("row", "col"), None, None),
        P("row", "col", None, None),
    )
    return jax.shard_map(
        functools.partial(shards, (mesh.shape["row"], mesh.shape["col"])),
        mesh=mesh,
        in_specs=placed,
        out_specs=(P(("row", "col"), None, None), P(("row", "col"), None, None)),
        check_vma=False,
    )
```

time: 649 us -> 104 us (0.16)
  blocking collectives: 311 us -> 0 us
  local copies, waits for them, and re-layouts: 108 us -> 3.51 us
  Pallas kernels: 0 us -> 93.4 us
  other arithmetic: 88.9 us -> 5.73 us
  matrix products: 49 us -> 0 us
  loops' own time: 45.2 us -> 0.01 us
  waiting for transfers between devices: 27.9 us -> 0 us
  between operations: 15.2 us -> 1.4 us
    psum x5 -> x0, blocking collectives: 200 us -> none  [the longest x3 121 us: squares(): return lax.psum(jnp.sum(residual * residual, axis=(0, 2)), ('row', 'col'))]
    all_gather x6 -> x0, blocking collectives: 111 us -> none  [the longest x4 83.5 us: apply_operator(): pieces = lax.all_gather(vectors, 'col', axis=0, tiled=True)]
    gather x182 -> x0, local copies, waits for them, and re-layouts: 103 us -> none  [the longest x60 34.3 us: group_weights(): col_points[cols_group]]
    pallas_call x0 -> x2, Pallas kernels: none -> 93.4 us  [the longest x1 77.2 us: solve(): pl.pallas_call(functools.partial(solve_kernel, dims, groups), out_shape=[...]
    dot_general x60 -> x0, matrix products: 49 us -> none  [visit(): jnp.einsum('pab,psa->psb', weights, pieces[local_rows], precision=lax.Pre...]
    another operation x4 -> x1, loops' own time: 45.2 us -> 0.01 us  [shards(): lax.cond(largest <= small, functools.partial(solve, dims, small, 1), func...]
    convert_element_type x60 -> x4, other arithmetic: 38.1 us -> 0.69 us  [the longest x1 0.65 us: shards(): jnp.sum(group_ids[:, None] >= first[None, 1:], axis=1).astype(jnp.int32)]
    scatter-add x60 -> x0, other arithmetic: 36.6 us -> none  [visit(): return running.at[cols_group].add(product)]
  transfers between devices with their start and end apart: 4 -> 0, of which waited for: 4 -> 0; matrix products, arithmetic and copies ran while one was open for 0% -> 0% of each run, Pallas kernels for 0% -> 0%
where the time goes in v2:
time: 104 us
  Pallas kernels  93.4 us (90%)
  other arithmetic  5.73 us (6%)
  local copies, waits for them, and re-layouts  3.51 us (3%)
  between operations  1.4 us (1%)
    pallas_call x1, Pallas kernels, solve(): pl.pallas_call(functools.partial(solve_kernel, dims, groups), out_shape=[...  77.2 us
    pallas_call x1, Pallas kernels, all_gather(): pl.pallas_call(functools.partial(gather_kernel, dims), out_shape=jax.Shap...  16.1 us
    unnamed x11, local copies, waits for them, and re-layouts  2.59 us

profile of v2, /device:TPU:0, one launch (start us, length us, event | category | flops | bytes accessed | tf_op | source)
XLA Modules:
  0.0 104.0 jit_solution(13354137245406477131)
XLA Ops:
  0.6 0.0 copy-start.3
  0.6 0.7 copy-done.3
  1.4 16.1 %shard_map.79 = f32[32,2,8,256]{3,2,1,0:T(8,128)S(1)} custom-call(f32[2,8,256]{2,1,0:T(8,128)S(1)} %pad.4.refs_0_), custom_call_target="tpu_custom_call" | custom-call | tf_op jit(solution)/shard_map/pallas_call | solution.py:162
  17.5 0.3 fusion.10
  17.8 0.1 copy.33
  17.8 0.1 copy.32
  17.9 0.3 fusion
  18.2 0.1 convert_reduce_fusion
  18.3 0.1 dynamic_slice.7
  18.4 0.1 fusion.7
  18.5 0.6 slice.3
  19.1 0.6 compare_convert_fusion
  19.7 0.1 reduce_sum.61
  19.9 0.1 fusion.5
  20.0 0.6 reduce_max.19
  21.3 0.1 multiply_reduce_fusion
  21.4 0.1 compare_select_fusion.1
  21.5 0.0 copy-start
  21.5 0.0 copy-start.1
  21.5 0.0 copy-start.2
  21.5 0.7 copy-done
  22.2 0.0 copy-done.1
  22.2 0.0 copy-done.2
  22.2 80.5 %conditional.1 = ((f32[2,8,256]{2,1,0:T(8,128)S(1)}, f32[2,8,256]{2,1,0:T(8,128)S(1)})) conditional(s32[]{:T(128)} %convert_element_type.27, (pred[56,2,64]{2,1,0:T(4,128)(4,1)S(1)}, s32[56,2,64]{2,1,0:T(2,128)S(1)}, s32[14]{0:T(128)S(1)}, f32[32,2,8,256]{3,2,1,0:T(8,128)S(1)}, f32[2,8,256]{2,1,0:T(8,128)S(1)}, ...), branch_computations={%region_10.11_spmd.clone, %region_11.12_spmd.clone} | conditional | flops 21392 | bytes 64980 | solution.py:430
  22.2 1.6 %select_reduce_fusion.1.near_ref = s32[56]{0:T(128)} fusion(s32[]{:T(128)} %get-tuple-element.115, pred[56,2,64]{2,1,0:T(4,128)(4,1)S(1)} %get-tuple-element.119, s32[56,2,64]{2,1,0:T(2,128)S(1)} %get-tuple-element.120, s32[]{:T(128)} %get-tuple-element.124), kind=kLoop, calls=%fused_computation.1 | loop fusion | flops 14280 | bytes 36072 | tf_op jit(solution)/shard_map/reduce_sum | solution.py:422
  23.9 1.7 %reduce_sum.74.valid_ref = s32[56]{0:T(128)} reduce(s32[56,2,64]{2,1,0:T(2,128)S(1)} %get-tuple-element.116, s32[]{:T(128)} %get-tuple-element.115), dimensions={1,2}, to_apply=%region_9.10.clone | reduce | flops 7112 | bytes 28900 | tf_op jit(solution)/shard_map/reduce_sum | solution.py:423
  25.5 77.2 %branch_1_fun.1 = (f32[2,8,256]{2,1,0:T(8,128)S(1)}, f32[2,8,256]{2,1,0:T(8,128)S(1)}) custom-call(s32[56]{0:T(128)} %select_reduce_fusion.1.near_ref, s32[56]{0:T(128)} %reduce_sum.74.valid_ref, s32[14]{0:T(128)S(1)} %get-tuple-element.111.side_ref, f32[64,8,256]{2,1,0:T(8,128)S(1)} %bitcast.6, f32[2,8,256]{2,1,0:T(8,128)S(1)} %get-tuple-element.112.own_points_ref, ...), custom_call_target="tpu_custom_call" | custom-call | tf_op jit(solution)/shard_map/cond/branch_1_fun/pallas_call | solution.py:373
  102.8 0.6 copy.40
  103.4 0.6 copy.41
  (9 shorter events, 0.1 us)
Async XLA Ops:
  0.6 0.7 copy-start.3
  21.5 0.7 copy-start
  21.5 0.7 copy-start.1
  21.5 0.7 copy-start.2

commit v3 on v2

--- a/solution.py
+++ b/solution.py
@@ -84,6 +84,7 @@
     for k in range(1, zs):
         for a in range(count):
             along_z[k, a] = send(a, ins[a], mine, device(x, (z + k) % zs, y, c))
+    yield
     for a in range(count):
         local[a].wait()
 
@@ -99,11 +100,13 @@
             ahead[k, a] = send(a, outs[a].at[place], place, device(x2, z, y2, c))
             aside[k, a] = send(a, outs[a].at[place], place, device(x3, z, y3, c))
             swaps.append(send(a, outs[a].at[place], place, other))
+        yield
         for k, a in steps:
             ahead[k, a].wait_recv()
             place = slot(x2, (z - k + zs) % zs, y2, c)
             late[k, a] = send(a, outs[a].at[place], place, device(x3, z, y3, c))
             swaps.append(send(a, outs[a].at[place], place, other))
+        yield
         for k, a in steps:
             aside[k, a].wait_recv()
             place = slot(x3, (z - k + zs) % zs, y3, c)
@@ -154,7 +157,8 @@
     for partner in partners:
         pl.semaphore_signal(barrier, inc=1, device_id=partner, device_id_type=MESH)
     pl.semaphore_wait(barrier, len(partners))
-    gather(dims, [in_ref], [out_ref], send_sem, recv_sem, local_sem)
+    for _ in gather(dims, [in_ref], [out_ref], send_sem, recv_sem, local_sem):
+        pass
 
 
 def all_gather(dims, collective_id, slab):
@@ -181,7 +185,7 @@
 
 def solve_kernel(
     dims, groups,
-    near_ref, valid_ref, side_ref, points_ref, own_points_ref, noise_ref, right_ref, guess_ref,
+    near_ref, side_ref, points_ref, own_points_ref, noise_ref, right_ref, guess_ref,
     field_out, residual_out,
     buffers, dir_ref, vectors_ref, blocks, outgoing, dot_ref, dots_ref,
     send_sem, recv_sem, local_sem, dot_send, dot_recv,
@@ -203,21 +207,24 @@
         return carry
 
     lax.fori_loop(1, devices, greet, 0)
-    pl.semaphore_wait(barrier, devices - 1)
-
-    def spread(number, source):
-        gather(
+
+    def spreading(number, source):
+        return gather(
             dims, [source], [buffers.at[number]],
             send_sem.at[number], recv_sem.at[number], local_sem.at[number],
         )
 
+    def spread(number, source):
+        for _ in spreading(number, source):
+            pass
+
     rows = 32
     block = 2 * tile
 
     def build(e, carry):
-        left = points_ref[near_ref[e]].T
+        left = points_ref[jnp.maximum(near_ref[e], 0)].T
         right = own_points_ref[side_ref[e // GROUP]]
-        reach = valid_ref[e].astype(jnp.float32)
+        reach = jnp.minimum(near_ref[e] + 1, 1).astype(jnp.float32)
         for chunk in range(tile // rows):
             squared = None
             for component in range(3):
@@ -243,7 +250,7 @@
         def step(g, totals):
             parts = []
             for i in range(GROUP):
-                part = vectors_ref[near_ref[g * GROUP + i]]
+                part = vectors_ref[jnp.maximum(near_ref[g * GROUP + i], 0)]
                 parts += [part, part]
             first = pl.multiple_of(g * GROUP * block, GROUP * block)
             term = jnp.dot(
@@ -270,8 +277,15 @@
     zero = jnp.zeros((rhs, tile), jnp.float32)
     noise = [noise_ref[p : p + 1, :] for p in range(own)]
 
-    lax.fori_loop(0, groups * GROUP, build, 0)
-    spread(0, guess_ref)
+    shares = 5
+    bounds = [groups * GROUP * i // shares for i in range(shares + 1)]
+    lax.fori_loop(bounds[0], bounds[1], build, 0)
+    pl.semaphore_wait(barrier, devices - 1)
+    built = 1
+    for _ in spreading(0, guess_ref):
+        lax.fori_loop(bounds[built], bounds[built + 1], build, 0)
+        built += 1
+    lax.fori_loop(bounds[built], bounds[shares], build, 0)
 
     def take_guess(i, p, carry):
         vectors_ref[i * own + p] = split_rows(buffers[0, i, p])
@@ -365,7 +379,7 @@
 
 def solve(dims, groups, collective_id, *operands):
     devices = dims[0] * dims[1] * dims[2] * dims[3]
-    points, right = operands[3], operands[6]
+    points, right = operands[2], operands[5]
     tiles, tile = points.shape[0], points.shape[2]
     own, rhs, _ = right.shape
     dma = pltpu.SemaphoreType.DMA
@@ -373,7 +387,7 @@
     return pl.pallas_call(
         functools.partial(solve_kernel, dims, groups),
         out_shape=[jax.ShapeDtypeStruct(right.shape, jnp.float32)] * 2,
-        in_specs=[SMEM_SPEC] * 3 + [VMEM_SPEC] * 5,
+        in_specs=[SMEM_SPEC] * 2 + [VMEM_SPEC] * 5,
         out_specs=[VMEM_SPEC] * 2,
         scratch_shapes=[
             pltpu.VMEM((phases, devices, own, rhs, tile), jnp.float32),
@@ -418,13 +432,14 @@
     goal = jnp.where(own_near > 0, rank + first[:, None] * GROUP, -1)
     capacity = own * CAPACITY
     slots = jnp.arange(capacity, dtype=jnp.int32)
-    hit = goal[None] == slots[:, None, None]
-    near_ids = jnp.sum(jnp.where(hit, ids[None, None, :], 0), axis=(1, 2)).astype(jnp.int32)
-    valid = jnp.sum(hit, axis=(1, 2)).astype(jnp.int32)
+    hit = goal.reshape(1, own * tiles) == slots[:, None]
+    known = jnp.tile(ids + 1, own)[None]
+    near_ids = (jnp.sum(jnp.where(hit, known, 0), axis=1) - 1).astype(jnp.int32)
     group_ids = jnp.arange(capacity // GROUP, dtype=jnp.int32)
     side = jnp.sum(group_ids[:, None] >= first[None, 1:], axis=1).astype(jnp.int32)
 
-    operands = (near_ids, valid, side, points, padded, noise_var, right_side, start_guess)
+    near_ids, side, largest = lax.optimization_barrier((near_ids, side, largest))
+    operands = (near_ids, side, points, padded, noise_var, right_side, start_guess)
     small = own * 4
     return tuple(
         lax.cond(

time: 104 us -> 90.8 us (0.87)
  Pallas kernels: 93.4 us -> 83.7 us
  other arithmetic: 5.73 us -> 2.51 us
    pallas_call x1, Pallas kernels: 77.2 us -> 67.6 us  [solve(): pl.pallas_call(functools.partial(solve_kernel, dims, groups), out_shape=[...]
    reduce_sum x2 -> x1, other arithmetic: 3.31 us -> 0.11 us  [shards(): near_ids = (jnp.sum(jnp.where(hit, known, 0), axis=1) - 1).astype(jnp.int32)]
    unnamed x11 -> x9, local copies, waits for them, and re-layouts: 2.59 us -> 1.92 us
where the time goes in v3:
time: 90.8 us; the launch traced here: 90.6 us
  Pallas kernels  83.7 us (92%)
  local copies, waits for them, and re-layouts  2.99 us (3%)
  other arithmetic  2.51 us (3%)
  between operations  1.43 us (2%)
    pallas_call x1, Pallas kernels, solve(): pl.pallas_call(functools.partial(solve_kernel, dims, groups), out_shape=[...  67.6 us
    pallas_call x1, Pallas kernels, all_gather(): pl.pallas_call(functools.partial(gather_kernel, dims), out_shape=jax.Shap...  16.1 us
    unnamed x9, local copies, waits for them, and re-layouts  1.92 us

profile of v3, /device:TPU:0, one launch (start us, length us, event | category | flops | bytes accessed | tf_op | source)
XLA Modules:
  0.0 90.6 jit_solution(4317970765403393609)
XLA Ops:
  0.6 0.7 copy.21
  1.3 16.1 %shard_map.69 = f32[32,2,8,256]{3,2,1,0:T(8,128)S(1)} custom-call(f32[2,8,256]{2,1,0:T(8,128)S(1)} %pad.4.refs_0_), custom_call_target="tpu_custom_call" | custom-call | tf_op jit(solution)/shard_map/pallas_call | solution.py:166
  17.4 0.3 fusion.9
  17.7 0.1 copy.22
  17.7 0.1 copy.23
  17.8 0.3 fusion
  18.0 0.1 convert_reduce_fusion
  18.2 0.1 dynamic_slice.7
  18.3 0.1 fusion.7
  18.4 0.1 multiply_reduce_fusion
  18.5 0.1 compare_select_fusion.1
  18.6 0.1 eq.15
  18.7 0.1 broadcast_in_dim.15
  18.8 0.1 select_reduce_fusion
  18.9 0.6 slice.3
  19.5 0.6 compare_convert_fusion
  20.2 0.0 copy-start
  20.2 0.0 copy-start.1
  20.2 0.1 reduce_sum.55
  20.3 0.1 fusion.5
  20.4 0.6 reduce_max.19
  21.1 0.0 copy-start.2
  21.7 0.0 copy-done
  21.7 0.0 copy-done.1
  21.8 0.0 copy-done.2
  21.8 67.7 %conditional.1 = ((f32[2,8,256]{2,1,0:T(8,128)S(1)}, f32[2,8,256]{2,1,0:T(8,128)S(1)})) conditional(s32[]{:T(128)} %convert_element_type.26, (s32[56]{0:T(128)S(1)}, s32[14]{0:T(128)S(1)}, f32[32,2,8,256]{3,2,1,0:T(8,128)S(1)}, f32[2,8,256]{2,1,0:T(8,128)S(1)}, f32[2,256]{1,0:T(2,128)S(1)}, /*index=5*/f32[2,8,256]{2,1,0:T(8,128)S(1)}, ...), branch_computations={%region_9.10_spmd, %region_10.11_spmd} | conditional | bytes 8 | solution.py:445
  21.8 67.6 %branch_1_fun.1 = (f32[2,8,256]{2,1,0:T(8,128)S(1)}, f32[2,8,256]{2,1,0:T(8,128)S(1)}) custom-call(s32[56]{0:T(128)S(1)} %get-tuple-element.35.near_ref, s32[14]{0:T(128)S(1)} %get-tuple-element.36.side_ref, f32[64,8,256]{2,1,0:T(8,128)S(1)} %bitcast.6, f32[2,8,256]{2,1,0:T(8,128)S(1)} %get-tuple-element.38.own_points_ref, ...), custom_call_target="tpu_custom_call" | custom-call | tf_op jit(solution)/shard_map/cond/branch_1_fun/pallas_call | solution.py:387
  89.4 0.6 copy.30
  90.0 0.6 copy.31
  (9 shorter events, 0.1 us)
Async XLA Ops:
  20.2 1.6 %copy-start = (f32[2,8,256]{2,1,0:T(8,128)S(1)}, f32[2,8,256]{2,1,0:T(8,128)}, u32[]{:S(2)}) copy-start(f32[2,8,256]{2,1,0:T(8,128)} %param.9) | copy-start | bytes 49156
  20.2 1.6 %copy-start.1 = (f32[2,8,256]{2,1,0:T(8,128)S(1)}, f32[2,8,256]{2,1,0:T(8,128)}, u32[]{:S(2)}) copy-start(f32[2,8,256]{2,1,0:T(8,128)} %param.10) | copy-start | bytes 49156
  21.1 0.7 copy-start.2

commit v4 on v3

--- a/solution.py
+++ b/solution.py
@@ -34,10 +34,22 @@
     return x, col // (ys * cs), (col // cs) % ys, col % cs
 
 
+def flip(index, k, size):
+    if size & (size - 1):
+        return (k - index + 2 * size) % size
+    result, bit = 0, 1
+    while bit < size:
+        result = result + (index // bit + k // bit) % 2 * bit
+        bit *= 2
+    return result
+
+
 def gather_partners(dims):
     xs, zs, ys, cs = dims
     x, z, y, c = position(dims)
     partners = [(x, (((z + k) % zs) * ys + y) * cs + c) for k in range(1, zs)]
+    if xs == 2 and ys == 2:
+        partners += [(1 - x, (z * ys + 1 - y) * cs + c)]
     partners += [(x, (z * ys + (y + k) % ys) * cs + c) for k in range(1, ys)]
     partners += [((x + k) % xs, (z * ys + y) * cs + c) for k in range(1, xs)]
     partners += [(x, (z * ys + y) * cs + 1 - c)]
@@ -81,40 +93,33 @@
     mine = slot(x, z, y, c)
     other = device(x, z, y, 1 - c)
     along_z = {}
-    for k in range(1, zs):
+    for k in reversed(range(1, zs)):
         for a in range(count):
-            along_z[k, a] = send(a, ins[a], mine, device(x, (z + k) % zs, y, c))
+            along_z[k, a] = send(a, ins[a], mine, device(x, flip(z, k, zs), y, c))
     yield
     for a in range(count):
         local[a].wait()
 
     if xs == 2 and ys == 2:
-        x2, y2 = (x + c) % 2, (y + 1 - c) % 2
-        x3, y3 = (x + 1 - c) % 2, (y + c) % 2
-        ahead, aside, late, swaps = {}, {}, {}, []
-        steps = [(k, a) for k in range(zs) for a in range(count)]
-        for k, a in steps:
-            if k:
-                along_z[k, a].wait_recv()
-            place = slot(x, (z - k + zs) % zs, y, c)
-            ahead[k, a] = send(a, outs[a].at[place], place, device(x2, z, y2, c))
-            aside[k, a] = send(a, outs[a].at[place], place, device(x3, z, y3, c))
-            swaps.append(send(a, outs[a].at[place], place, other))
+        across_by = ((1 - x, 1 - y), ((x + c) % 2, (y + 1 - c) % 2), ((x + 1 - c) % 2, (y + c) % 2))
+        arrivals, swaps = [], []
+        for k in range(zs):
+            level = flip(z, k, zs)
+            for a in range(count):
+                if k:
+                    along_z[k, a].wait_recv()
+                place = slot(x, level, y, c)
+                for xx, yy in across_by:
+                    copy = send(a, outs[a].at[place], place, device(xx, z, yy, c))
+                    arrivals.append((copy, a, slot(xx, level, yy, c)))
+                swaps.append(send(a, outs[a].at[place], place, other))
         yield
-        for k, a in steps:
-            ahead[k, a].wait_recv()
-            place = slot(x2, (z - k + zs) % zs, y2, c)
-            late[k, a] = send(a, outs[a].at[place], place, device(x3, z, y3, c))
-            swaps.append(send(a, outs[a].at[place], place, other))
-        yield
-        for k, a in steps:
-            aside[k, a].wait_recv()
-            place = slot(x3, (z - k + zs) % zs, y3, c)
-            swaps.append(send(a, outs[a].at[place], place, other))
-        for k, a in steps:
-            late[k, a].wait_recv()
-            place = slot(1 - x, (z - k + zs) % zs, 1 - y, c)
-            swaps.append(send(a, outs[a].at[place], place, other))
+        for number, way in enumerate((1, 2, 0)):
+            for copy, a, place in arrivals[way::3]:
+                copy.wait_recv()
+                swaps.append(send(a, outs[a].at[place], place, other))
+            if number == 1:
+                yield
         for copy in swaps:
             copy.wait_recv()
         for copy in sent:
@@ -272,7 +277,7 @@
         def one(i, carry):
             return body(i // own, i % own, carry)
 
-        return lax.fori_loop(0, tiles, one, start, unroll=8)
+        return lax.fori_loop(0, tiles, one, start, unroll=16)
 
     zero = jnp.zeros((rhs, tile), jnp.float32)
     noise = [noise_ref[p : p + 1, :] for p in range(own)]

time: 90.8 us -> 81.6 us (0.90)
  Pallas kernels: 83.7 us -> 74.2 us
    pallas_call x1, Pallas kernels: 67.6 us -> 60.4 us  [solve(): pl.pallas_call(functools.partial(solve_kernel, dims, groups), out_shape=[...]
    pallas_call x1, Pallas kernels: 16.1 us -> 13.8 us  [all_gather(): pl.pallas_call(functools.partial(gather_kernel, dims), out_shape=jax.Shap...]
where the time goes in v4:
time: 81.6 us; the launch traced here: 81.4 us
  Pallas kernels  74.2 us (91%)
  local copies, waits for them, and re-layouts  2.99 us (4%)
  other arithmetic  2.51 us (3%)
  between operations  1.43 us (2%)
    pallas_call x1, Pallas kernels, solve(): pl.pallas_call(functools.partial(solve_kernel, dims, groups), out_shape=[...  60.4 us
    pallas_call x1, Pallas kernels, all_gather(): pl.pallas_call(functools.partial(gather_kernel, dims), out_shape=jax.Shap...  13.8 us
    unnamed x9, local copies, waits for them, and re-layouts  1.92 us

profile of v4, /device:TPU:0, one launch (start us, length us, event | category | flops | bytes accessed | tf_op | source)
XLA Modules:
  0.0 81.4 jit_solution(17198299283875453037)
XLA Ops:
  0.6 0.7 copy.21
  1.3 13.8 %shard_map.69 = f32[32,2,8,256]{3,2,1,0:T(8,128)S(1)} custom-call(f32[2,8,256]{2,1,0:T(8,128)S(1)} %pad.4.refs_0_), custom_call_target="tpu_custom_call" | custom-call | tf_op jit(solution)/shard_map/pallas_call | solution.py:171
  15.1 0.3 fusion.9
  15.4 0.1 copy.22
  15.5 0.1 copy.23
  15.5 0.3 fusion
  15.8 0.1 convert_reduce_fusion
  15.9 0.1 dynamic_slice.7
  16.0 0.1 fusion.7
  16.2 0.1 multiply_reduce_fusion
  16.3 0.1 compare_select_fusion.1
  16.4 0.1 eq.15
  16.5 0.1 broadcast_in_dim.15
  16.5 0.1 select_reduce_fusion
  16.7 0.6 slice.3
  17.2 0.6 compare_convert_fusion
  17.9 0.0 copy-start
  17.9 0.0 copy-start.1
  17.9 0.1 reduce_sum.55
  18.0 0.1 fusion.5
  18.2 0.6 reduce_max.19
  18.8 0.0 copy-start.2
  19.5 0.0 copy-done
  19.5 0.0 copy-done.1
  19.5 0.0 copy-done.2
  19.5 60.6 %conditional.1 = ((f32[2,8,256]{2,1,0:T(8,128)S(1)}, f32[2,8,256]{2,1,0:T(8,128)S(1)})) conditional(s32[]{:T(128)} %convert_element_type.26, (s32[56]{0:T(128)S(1)}, s32[14]{0:T(128)S(1)}, f32[32,2,8,256]{3,2,1,0:T(8,128)S(1)}, f32[2,8,256]{2,1,0:T(8,128)S(1)}, f32[2,256]{1,0:T(2,128)S(1)}, /*index=5*/f32[2,8,256]{2,1,0:T(8,128)S(1)}, ...), branch_computations={%region_9.10_spmd, %region_10.11_spmd} | conditional | bytes 8 | solution.py:450
  19.7 60.4 %branch_1_fun.1 = (f32[2,8,256]{2,1,0:T(8,128)S(1)}, f32[2,8,256]{2,1,0:T(8,128)S(1)}) custom-call(s32[56]{0:T(128)S(1)} %get-tuple-element.35.near_ref, s32[14]{0:T(128)S(1)} %get-tuple-element.36.side_ref, f32[64,8,256]{2,1,0:T(8,128)S(1)} %bitcast.6, f32[2,8,256]{2,1,0:T(8,128)S(1)} %get-tuple-element.38.own_points_ref, ...), custom_call_target="tpu_custom_call" | custom-call | tf_op jit(solution)/shard_map/cond/branch_1_fun/pallas_call | solution.py:392
  80.1 0.6 copy.30
  80.8 0.6 copy.31
  (9 shorter events, 0.1 us)
Async XLA Ops:
  17.9 1.6 %copy-start = (f32[2,8,256]{2,1,0:T(8,128)S(1)}, f32[2,8,256]{2,1,0:T(8,128)}, u32[]{:S(2)}) copy-start(f32[2,8,256]{2,1,0:T(8,128)} %param.9) | copy-start | bytes 49156
  17.9 1.6 %copy-start.1 = (f32[2,8,256]{2,1,0:T(8,128)S(1)}, f32[2,8,256]{2,1,0:T(8,128)}, u32[]{:S(2)}) copy-start(f32[2,8,256]{2,1,0:T(8,128)} %param.10) | copy-start | bytes 49156
  18.8 0.7 copy-start.2

commit v5 on v4

--- a/solution.py
+++ b/solution.py
@@ -270,7 +270,7 @@
             )
 
         start = tuple(jnp.zeros((2 * rhs, tile), jnp.float32) for _ in range(own))
-        totals = lax.fori_loop(0, groups, step, start, unroll=2)
+        totals = lax.fori_loop(0, groups, step, start, unroll=4 if groups % 4 == 0 else 2)
         return [total[:rhs] + total[rhs:] for total in totals]
 
     def over_tiles(body, start):
@@ -283,14 +283,14 @@
     noise = [noise_ref[p : p + 1, :] for p in range(own)]
 
     shares = 5
-    bounds = [groups * GROUP * i // shares for i in range(shares + 1)]
-    lax.fori_loop(bounds[0], bounds[1], build, 0)
+    bounds = [groups * GROUP // 2 * i // shares * 2 for i in range(shares + 1)]
+    lax.fori_loop(bounds[0], bounds[1], build, 0, unroll=2)
     pl.semaphore_wait(barrier, devices - 1)
     built = 1
     for _ in spreading(0, guess_ref):
-        lax.fori_loop(bounds[built], bounds[built + 1], build, 0)
+        lax.fori_loop(bounds[built], bounds[built + 1], build, 0, unroll=2)
         built += 1
-    lax.fori_loop(bounds[built], bounds[shares], build, 0)
+    lax.fori_loop(bounds[built], bounds[shares], build, 0, unroll=2)
 
     def take_guess(i, p, carry):
         vectors_ref[i * own + p] = split_rows(buffers[0, i, p])

time: 81.6 us -> 79.2 us (0.971)
  Pallas kernels: 74.2 us -> 71.8 us
    pallas_call x1, Pallas kernels: 60.4 us -> 58 us  [solve(): pl.pallas_call(functools.partial(solve_kernel, dims, groups), out_shape=[...]
where the time goes in v5:
time: 79.2 us; the launch traced here: 79 us
  Pallas kernels  71.8 us (91%)
  local copies, waits for them, and re-layouts  2.99 us (4%)
  other arithmetic  2.51 us (3%)
  between operations  1.43 us (2%)
    pallas_call x1, Pallas kernels, solve(): pl.pallas_call(functools.partial(solve_kernel, dims, groups), out_shape=[...  58 us
    pallas_call x1, Pallas kernels, all_gather(): pl.pallas_call(functools.partial(gather_kernel, dims), out_shape=jax.Shap...  13.8 us
    unnamed x9, local copies, waits for them, and re-layouts  1.92 us

profile of v5, /device:TPU:0, one launch (start us, length us, event | category | flops | bytes accessed | tf_op | source)
XLA Modules:
  0.0 79.0 jit_solution(17753346779281548308)
XLA Ops:
  0.6 0.7 copy.21
  1.3 13.8 %shard_map.69 = f32[32,2,8,256]{3,2,1,0:T(8,128)S(1)} custom-call(f32[2,8,256]{2,1,0:T(8,128)S(1)} %pad.4.refs_0_), custom_call_target="tpu_custom_call" | custom-call | tf_op jit(solution)/shard_map/pallas_call | solution.py:171
  15.1 0.3 fusion.9
  15.4 0.1 copy.22
  15.5 0.1 copy.23
  15.5 0.3 fusion
  15.8 0.1 convert_reduce_fusion
  15.9 0.1 dynamic_slice.7
  16.0 0.1 fusion.7
  16.2 0.1 multiply_reduce_fusion
  16.3 0.1 compare_select_fusion.1
  16.4 0.1 eq.15
  16.5 0.1 broadcast_in_dim.15
  16.5 0.1 select_reduce_fusion
  16.7 0.6 slice.3
  17.2 0.6 compare_convert_fusion
  17.9 0.0 copy-start
  17.9 0.0 copy-start.1
  17.9 0.1 reduce_sum.55
  18.0 0.1 fusion.5
  18.2 0.6 reduce_max.19
  18.8 0.0 copy-start.2
  19.5 0.0 copy-done
  19.5 0.0 copy-done.1
  19.5 0.0 copy-done.2
  19.5 58.2 %conditional.1 = ((f32[2,8,256]{2,1,0:T(8,128)S(1)}, f32[2,8,256]{2,1,0:T(8,128)S(1)})) conditional(s32[]{:T(128)} %convert_element_type.26, (s32[56]{0:T(128)S(1)}, s32[14]{0:T(128)S(1)}, f32[32,2,8,256]{3,2,1,0:T(8,128)S(1)}, f32[2,8,256]{2,1,0:T(8,128)S(1)}, f32[2,256]{1,0:T(2,128)S(1)}, /*index=5*/f32[2,8,256]{2,1,0:T(8,128)S(1)}, ...), branch_computations={%region_9.10_spmd, %region_10.11_spmd} | conditional | bytes 8 | solution.py:450
  19.7 58.0 %branch_1_fun.1 = (f32[2,8,256]{2,1,0:T(8,128)S(1)}, f32[2,8,256]{2,1,0:T(8,128)S(1)}) custom-call(s32[56]{0:T(128)S(1)} %get-tuple-element.35.near_ref, s32[14]{0:T(128)S(1)} %get-tuple-element.36.side_ref, f32[64,8,256]{2,1,0:T(8,128)S(1)} %bitcast.6, f32[2,8,256]{2,1,0:T(8,128)S(1)} %get-tuple-element.38.own_points_ref, ...), custom_call_target="tpu_custom_call" | custom-call | tf_op jit(solution)/shard_map/cond/branch_1_fun/pallas_call | solution.py:392
  77.7 0.6 copy.30
  78.4 0.6 copy.31
  (9 shorter events, 0.1 us)
Async XLA Ops:
  17.9 1.6 %copy-start = (f32[2,8,256]{2,1,0:T(8,128)S(1)}, f32[2,8,256]{2,1,0:T(8,128)}, u32[]{:S(2)}) copy-start(f32[2,8,256]{2,1,0:T(8,128)} %param.9) | copy-start | bytes 49156
  17.9 1.6 %copy-start.1 = (f32[2,8,256]{2,1,0:T(8,128)S(1)}, f32[2,8,256]{2,1,0:T(8,128)}, u32[]{:S(2)}) copy-start(f32[2,8,256]{2,1,0:T(8,128)} %param.10) | copy-start | bytes 49156
  18.8 0.7 copy-start.2
